TPU v7x, 512 devices: a whole 4x8x8 slice. The times are simulated.
512 devices in a mesh: node: 64 (over y_lo, z, core), win: 8 (over y_hi, x).
Axes of the slice: x: 4, y: 8 (y_hi: 2, y_lo: 4; y = y_hi * 4 + y_lo), z: 8, core: 2. Of those that a mesh axis runs over, the one named last changes fastest.
Arguments:
- features: bfloat16 [32768, 8, 2, 128], P('node', 'win'), may hold values from -6 to 6
- node_vectors: float32 [32768, 128], P('node'), may hold values from -0.3 to 0.3
- projections: float32 [2, 64, 64], replicated, may hold values from -0.75 to 0.75
- mix_weight: bfloat16 [3, 128, 128], replicated, may hold values from -0.3125 to 0.3125
- region_sizes: int32 [128], replicated, may hold values from 1 to 4, 256 in all
- cotangent: bfloat16 [32768, 8, 2, 128], P('node', 'win'), may hold values from -6 to 6
Outputs:
- layer_output: bfloat16 [32768, 8, 2, 128], P('node', 'win')
- vector_grad: float32 [32768, 128], P('node')
- weight_grad: float32 [3, 128, 128], replicated
Inputs may be any that keep to these rules, and one draw needn't show every extreme that they name: `region_sizes`: each entry is a region size in units of 128 nodes; the entries sum to 256, and the largest region has 512 nodes.
All inputs are finite; a program needn't handle non-finite values.
Results may differ from a plain program's by a relative error of at most 0.015.
Values may be sent and summed in bfloat16 or wider, within the bound.
No kernel may reach another device: no remote copies, remote signals or barrier semaphores. Data moves between devices by JAX's collectives and lax.ppermute only.
A program may use at most 64 MiB of HBM per device.

v0:
```python
from functools import partial
import math
import jax
import jax.numpy as jnp
from jax import lax
from jax.sharding import PartitionSpec as P

BLOCK = 128
KEEP_INPUT = 0.05
ROWS_DIMS = (((1,), (1,)), ((), ()))
COLS_DIMS = (((0,), (0,)), ((), ()))


def padded(cells, sides, width):
    for axis, dim in sides:
        count = lax.axis_size(axis)
        ends = count - 1
        head = lax.slice_in_dim(cells, 0, width, axis=dim)
        tail = lax.slice_in_dim(cells, cells.shape[dim] - width, cells.shape[dim], axis=dim)
        cells = jnp.concatenate(
            [
                lax.ppermute(tail, axis, [(i, (i + 1) % count) for i in range(ends)]),
                cells,
                lax.ppermute(head, axis, [((i + 1) % count, i) for i in range(ends)]),
            ],
            axis=dim,
        )
    return cells


def shifted(block, axis, distance):
    devices = range(lax.axis_size(axis))
    route = [(i - distance, i) for i in devices if i - distance in devices]
    return lax.ppermute(block, axis, route)


def swapped(vectors):
    emb_half = vectors.shape[1] // 2
    return jnp.concatenate([vectors[:, emb_half:], -vectors[:, :emb_half]], axis=1)


def node_regions(region_sizes, node_index, node_total):
    region_ends = jnp.cumsum(region_sizes) * BLOCK
    region_index = jnp.sum((region_ends[None, :] <= node_index[:, None]).astype(jnp.int32), axis=1)
    in_range = (node_index >= 0) & (node_index < node_total)
    return jnp.where(in_range, region_index, -1)


def node_rim(values):
    return padded(values, (("node", 0),), values.shape[0])


def node_pass(values, offset_by):
    return shifted(values.astype(jnp.bfloat16), "node", offset_by).astype(values.dtype)


def spread_back(parts, node_count):
    lower = parts[:node_count]
    middle = parts[node_count : 2 * node_count]
    upper = parts[2 * node_count :]
    return middle + node_pass(lower, -1) + node_pass(upper, 1)


def dense_product(adj_rounded, wide_rows):
    return jnp.dot(adj_rounded, wide_rows, preferred_element_type=jnp.float32)


def body(features, node_vectors, projections, mix_weight, region_sizes, cotangent):
    node_count = features.shape[0]
    windows_dev = features.shape[1]
    steps_dev = features.shape[2]
    channels = features.shape[3]
    row_width = windows_dev * steps_dev * channels
    emb_half = node_vectors.shape[1] // 2
    node_total = node_count * lax.axis_size("node")
    first_node = lax.axis_index("node") * node_count
    own_index = first_node + jnp.arange(node_count, dtype=jnp.int32)
    wide_index = first_node - node_count + jnp.arange(3 * node_count, dtype=jnp.int32)
    own_region = node_regions(region_sizes, own_index, node_total)
    wide_region = node_regions(region_sizes, wide_index, node_total)
    highest = lax.Precision.HIGHEST
    source_m = jnp.tanh(
        3.0
        * jnp.dot(
            node_vectors[:, :emb_half],
            projections[0],
            precision=highest,
            preferred_element_type=jnp.float32,
        )
    )
    target_m = jnp.tanh(
        3.0
        * jnp.dot(
            node_vectors[:, emb_half:],
            projections[1],
            precision=highest,
            preferred_element_type=jnp.float32,
        )
    )
    learned = jnp.concatenate([source_m, target_m], axis=1).astype(jnp.bfloat16)
    inputs = features.reshape(node_count, row_width)
    rim_block = node_rim(jnp.concatenate([inputs, learned], axis=1))
    wide_inputs = rim_block[:, :row_width]
    wide_learned = rim_block[:, row_width:]
    scores = lax.dot_general(
        learned, swapped(wide_learned), ROWS_DIMS, preferred_element_type=jnp.float32
    )
    same_region = (own_region[:, None] == wide_region[None, :]) & (wide_region[None, :] >= 0)
    squashed = jnp.tanh(3.0 * scores)
    positive = jnp.maximum(squashed, 0.0)
    adjacency = jnp.where(same_region, positive * positive, 0.0)
    degree = 1.0 + jnp.sum(adjacency, axis=1)
    identity = (own_index[:, None] == wide_index[None, :]).astype(jnp.float32)
    adj_rounded = (adjacency + identity).astype(jnp.bfloat16)
    propagate = partial(dense_product, adj_rounded)
    inputs_f = inputs.astype(jnp.float32)
    prop_one = propagate(wide_inputs) / degree[:, None]
    hop_one = (KEEP_INPUT * inputs_f + (1.0 - KEEP_INPUT) * prop_one).astype(jnp.bfloat16)
    wide_one = node_rim(hop_one)
    prop_two = propagate(wide_one) / degree[:, None]
    hop_two = (KEEP_INPUT * inputs_f + (1.0 - KEEP_INPUT) * prop_two).astype(jnp.bfloat16)
    row_count = node_count * windows_dev * steps_dev
    hop_list = (inputs, hop_one, hop_two)
    mixed = jnp.zeros((row_count, channels), jnp.float32)
    for hop_order in range(3):
        mixed = mixed + jnp.dot(
            hop_list[hop_order].reshape(row_count, channels),
            mix_weight[hop_order],
            preferred_element_type=jnp.float32,
        )
    layer_output = mixed.astype(jnp.bfloat16).reshape(features.shape)
    upstream = cotangent.reshape(row_count, channels)
    norm_scale = 1.0 / math.sqrt(row_count * lax.axis_size("node") * lax.axis_size("win"))
    partial_mix = (
        jnp.stack(
            [
                lax.dot_general(
                    layer_rows.reshape(row_count, channels),
                    upstream,
                    COLS_DIMS,
                    preferred_element_type=jnp.float32,
                )
                for layer_rows in hop_list
            ]
        )
        * norm_scale
    )
    weight_grad = lax.psum(partial_mix, ("node", "win"))
    back_two = lax.dot_general(
        upstream, mix_weight[2], ROWS_DIMS, preferred_element_type=jnp.float32
    ).reshape(node_count, row_width)
    grad_two = ((1.0 - KEEP_INPUT) * back_two / degree[:, None]).astype(jnp.bfloat16)
    partials = lax.dot_general(adj_rounded, grad_two, COLS_DIMS, preferred_element_type=jnp.float32)
    carried = spread_back(partials, node_count)
    back_one = (
        lax.dot_general(
            upstream, mix_weight[1], ROWS_DIMS, preferred_element_type=jnp.float32
        ).reshape(node_count, row_width)
        + carried
    )
    grad_one = ((1.0 - KEEP_INPUT) * back_one / degree[:, None]).astype(jnp.bfloat16)
    pair_inner = lax.dot_general(
        jnp.concatenate([grad_one, grad_two], axis=1),
        jnp.concatenate([wide_inputs, wide_one], axis=1),
        ROWS_DIMS,
        preferred_element_type=jnp.float32,
    )
    offset = jnp.sum(grad_one.astype(jnp.float32) * prop_one, axis=1) + jnp.sum(
        grad_two.astype(jnp.float32) * prop_two, axis=1
    )
    score_grad = jnp.where(
        same_region,
        6.0 * (pair_inner - offset[:, None]) * positive * (1.0 - squashed * squashed),
        0.0,
    ).astype(jnp.bfloat16)
    row_part = jnp.dot(score_grad, swapped(wide_learned), preferred_element_type=jnp.float32)
    column_part = -lax.dot_general(
        score_grad, swapped(learned), COLS_DIMS, preferred_element_type=jnp.float32
    )
    grad_m = row_part + spread_back(column_part, node_count)
    source_grad = jnp.dot(
        3.0 * (1.0 - source_m * source_m) * grad_m[:, :emb_half],
        projections[0].T,
        precision=highest,
        preferred_element_type=jnp.float32,
    )
    target_grad = jnp.dot(
        3.0 * (1.0 - target_m * target_m) * grad_m[:, emb_half:],
        projections[1].T,
        precision=highest,
        preferred_element_type=jnp.float32,
    )
    vector_grad = lax.psum(
        jnp.concatenate([source_grad, target_grad], axis=1).astype(jnp.bfloat16), "win"
    ).astype(jnp.float32)
    return (layer_output, vector_grad, weight_grad)


def solution(mesh):
    placed = (
        P("node", "win", None, None),
        P("node", None),
        P(),
        P(),
        P(),
        P("node", "win", None, None),
    )
    return jax.shard_map(
        body,
        mesh=mesh,
        in_specs=placed,
        out_specs=(P("node", "win", None, None), P("node", None), P()),
        check_vma=False,
    )
```

profile of v0, /device:TPU:1, one launch (start us, length us, event | category | flops | bytes accessed | tf_op | source)
XLA Modules:
  0.0 480.1 jit_solution(4617464330748801811)
XLA Ops:
  7.2 2.1 fusion.88
  9.4 2.1 fusion.83
  12.8 8.8 %collective-permute-start.1 = (bf16[512,384]{1,0:T(8,128)(2,1)S(1)}, bf16[512,384]{1,0:T(8,128)(2,1)S(1)}, u32[]{:S(2)}, u32[]{:S(2)}) collective-permute-start(bf16[512,384]{1,0:T(8,128)(2,1)S(1)} %pad_maximum_fusion.1), channel_id=1, source_target_pairs={{8,0},{16,8},{24,16},{32,24},{40,32},{48,40},{56,48},{64,56},{72,6... | collective-permute-start | bytes 1179656 | tf_op jit(solution)/shard_map/ppermute | solution.py:24
  21.6 1.9 collective-permute-start
  25.7 2.5 collective-permute-done
  28.6 3.3 fusion.6
  32.0 1.5 add_convert_fusion.2
  33.5 1.9 collective-permute-start.3
  35.4 4.4 collective-permute-start.2
  43.4 3.5 multiply_reduce_fusion
  48.4 1.9 collective-permute-start.4
  50.3 4.4 collective-permute-start.5
  57.7 2.2 convolution_add_fusion.1
  59.9 1.6 multiply_reduce_fusion.1
  61.6 2.9 fusion.5
  64.6 1.3 fusion.90
  66.6 2.0 collective-permute-start.6
  68.6 3.6 collective-permute-start.7
  75.2 2.0 fusion.31
  81.1 1.7 fusion.14
  82.7 113.3 %all-reduce.3.cloned.1.call-done = bf16[512,128]{0,1:T(8,128)(2,1)} async-done(((bf16[512,128]{0,1:T(8,128)(2,1)}), bf16[512,128]{0,1:T(8,128)(2,1)}) %all-reduce.3.cloned.1.call-update) | async-done | bytes 131088 | tf_op jit(solution)/shard_map/psum | solution.py:193
  196.0 1.7 copy.38
  197.8 273.9 %all-reduce.5.cloned.1.call-done = f32[3,128,128]{2,1,0:T(8,128)} async-done(((f32[3,128,128]{2,1,0:T(8,128)}), f32[3,128,128]{2,1,0:T(8,128)}) %all-reduce.5.cloned.1.call-update) | async-done | bytes 196624 | tf_op jit(solution)/shard_map/psum | solution.py:148
  471.7 1.6 copy.54
  (103 shorter events, 19.4 us)
Async XLA Ops:
  7.2 17.5 %copy-start = (bf16[512,1,2,128]{3,2,1,0:T(2,128)(2,1)S(1)}, bf16[512,1,2,128]{3,2,1,0:T(2,128)(2,1)}, u32[]{:S(2)}) copy-start(bf16[512,1,2,128]{3,2,1,0:T(2,128)(2,1)} %param.11) | copy-start | bytes 786436
  7.2 16.4 %copy-start.26 = (s32[128]{0:T(128)S(1)}, s32[128]{0:T(128)}, u32[]{:S(2)}) copy-start(s32[128]{0:T(128)} %param.10) | copy-start | bytes 1540
  7.2 188.9 %all-reduce.3.cloned.1.call-start = ((), (), s32[]{:S(2)}) async-start(), calls=%async_computation | async-start | bytes 262144 | tf_op jit(solution)/shard_map/psum | solution.py:193
  9.4 19.2 %copy-start.10 = (bf16[512,64]{0,1:T(8,128)(2,1)}, bf16[512,64]{0,1:T(8,128)(2,1)S(1)}, u32[]{:S(2)}) copy-start(bf16[512,64]{0,1:T(8,128)(2,1)S(1)} %get-tuple-element.29) | copy-start | bytes 196612
  12.8 12.9 %collective-permute-start.1 = (bf16[512,384]{1,0:T(8,128)(2,1)S(1)}, bf16[512,384]{1,0:T(8,128)(2,1)S(1)}, u32[]{:S(2)}, u32[]{:S(2)}) collective-permute-start(bf16[512,384]{1,0:T(8,128)(2,1)S(1)} %pad_maximum_fusion.1), channel_id=1, source_target_pairs={{8,0},{16,8},{24,16},{32,24},{40,32},{48,40},{56,48},{64,56},{72,6... | collective-permute-start | bytes 1179656 | tf_op jit(solution)/shard_map/ppermute | solution.py:24
  21.6 6.6 %collective-permute-start = (bf16[512,384]{1,0:T(8,128)(2,1)S(1)}, bf16[512,384]{1,0:T(8,128)(2,1)S(1)}, u32[]{:S(2)}, u32[]{:S(2)}) collective-permute-start(bf16[512,384]{1,0:T(8,128)(2,1)S(1)} %pad_maximum_fusion.1), channel_id=1, source_target_pairs={{0,8},{8,16},{16,24},{24,32},{32,40},{40,48},{48,56},{56,64},{64,7... | collective-permute-start | bytes 1179656 | tf_op jit(solution)/shard_map/ppermute | solution.py:22
  28.4 28.2 %copy-start.1 = (bf16[1536,384]{1,0:T(8,128)(2,1)}, bf16[1536,384]{1,0:T(8,128)(2,1)S(1)}, u32[]{:S(2)}) copy-start(bf16[1536,384]{1,0:T(8,128)(2,1)S(1)} %pad_maximum_fusion) | copy-start | bytes 3538948
  32.0 7.8 %copy-start.14 = (bf16[3,128,128]{2,1,0:T(8,128)(2,1)S(1)}, bf16[3,128,128]{2,1,0:T(8,128)(2,1)}, u32[]{:S(2)}) copy-start(bf16[3,128,128]{2,1,0:T(8,128)(2,1)} %param.9) | copy-start | bytes 294916
  33.5 8.7 %collective-permute-start.3 = (bf16[512,256]{1,0:T(8,128)(2,1)}, bf16[512,256]{1,0:T(8,128)(2,1)}, u32[]{:S(2)}, u32[]{:S(2)}) collective-permute-start(bf16[512,256]{1,0:T(8,128)(2,1)} %get-tuple-element.33), channel_id=1, source_target_pairs={{8,0},{16,8},{24,16},{32,24},{40,32},{48,40},{56,48},{64,56},{72,6... | collective-permute-start | bytes 786440 | tf_op jit(solution)/shard_map/ppermute | solution.py:24
  35.4 8.0 %collective-permute-start.2 = (bf16[512,256]{1,0:T(8,128)(2,1)}, bf16[512,256]{1,0:T(8,128)(2,1)}, u32[]{:S(2)}, u32[]{:S(2)}) collective-permute-start(bf16[512,256]{1,0:T(8,128)(2,1)} %get-tuple-element.33), channel_id=1, source_target_pairs={{0,8},{8,16},{16,24},{24,32},{32,40},{40,48},{48,56},{56,64},{64,7... | collective-permute-start | bytes 786440 | tf_op jit(solution)/shard_map/ppermute | solution.py:22
  41.2 5.7 %copy-start.7 = (bf16[512,1536]{1,0:T(8,128)(2,1)S(1)}, bf16[512,1536]{1,0:T(8,128)(2,1)}, u32[]{:S(2)}) copy-start(bf16[512,1536]{1,0:T(8,128)(2,1)} %copy-done.6) | copy-start | bytes 4718596
  46.9 7.8 %copy-start.9 = (bf16[512,1,2,128]{3,2,1,0:T(2,128)(2,1)S(1)}, bf16[512,1,2,128]{3,2,1,0:T(2,128)(2,1)}, u32[]{:S(2)}) copy-start(bf16[512,1,2,128]{3,2,1,0:T(2,128)(2,1)} %param.6) | copy-start | bytes 786436
  48.4 11.6 %collective-permute-start.4 = (bf16[512,256]{1,0:T(8,128)(2,1)}, bf16[512,256]{1,0:T(8,128)(2,1)}, u32[]{:S(2)}, u32[]{:S(2)}) collective-permute-start(bf16[512,256]{1,0:T(8,128)(2,1)} %get-tuple-element.24), channel_id=1, source_target_pairs={{8,0},{16,8},{24,16},{32,24},{40,32},{48,40},{56,48},{64,56},{72,6... | collective-permute-start | bytes 786440 | tf_op jit(solution)/shard_map/ppermute | solution.py:34
  50.3 9.6 %collective-permute-start.5 = (bf16[512,256]{1,0:T(8,128)(2,1)}, bf16[512,256]{1,0:T(8,128)(2,1)}, u32[]{:S(2)}, u32[]{:S(2)}) collective-permute-start(bf16[512,256]{1,0:T(8,128)(2,1)} %get-tuple-element.25), channel_id=1, source_target_pairs={{0,8},{8,16},{16,24},{24,32},{32,40},{40,48},{48,56},{56,64},{64,7... | collective-permute-start | bytes 786440 | tf_op jit(solution)/shard_map/ppermute | solution.py:34
  64.5 8.6 %copy-start.18 = (bf16[512,256]{1,0:T(8,128)(2,1)S(1)}, bf16[512,256]{1,0:T(8,128)(2,1)}, u32[]{:S(2)}) copy-start(bf16[512,256]{1,0:T(8,128)(2,1)} %get-tuple-element.26) | copy-start | bytes 786436
  64.5 10.6 %copy-start.4 = (bf16[1536,64]{1,0:T(8,128)(2,1)S(1)}, bf16[1536,64]{1,0:T(8,128)(2,1)}, u32[]{:S(2)}) copy-start(bf16[1536,64]{1,0:T(8,128)(2,1)} %copy-done.3) | copy-start | bytes 589828
  65.8 11.3 %copy-start.13 = (f32[512,64]{0,1:T(8,128)S(1)}, f32[512,64]{0,1:T(8,128)}, u32[]{:S(2)}) copy-start(f32[512,64]{0,1:T(8,128)} %get-tuple-element.30) | copy-start | bytes 393220
  66.6 11.7 %copy-start.12 = (f32[512,64]{0,1:T(8,128)S(1)}, f32[512,64]{0,1:T(8,128)}, u32[]{:S(2)}) copy-start(f32[512,64]{0,1:T(8,128)} %get-tuple-element.31) | copy-start | bytes 393220
  66.6 6.7 %collective-permute-start.6 = (bf16[512,128]{0,1:T(8,128)(2,1)}, bf16[512,128]{0,1:T(8,128)(2,1)S(1)}, u32[]{:S(2)}, u32[]{:S(2)}) collective-permute-start(bf16[512,128]{0,1:T(8,128)(2,1)} %get-tuple-element.27), channel_id=1, source_target_pairs={{8,0},{16,8},{24,16},{32,24},{40,32},{48,40},{56,48},{64,56},{72,6... | collective-permute-start | bytes 393224 | tf_op jit(solution)/shard_map/ppermute | solution.py:34
  68.6 5.9 %collective-permute-start.7 = (bf16[512,128]{0,1:T(8,128)(2,1)}, bf16[512,128]{0,1:T(8,128)(2,1)S(1)}, u32[]{:S(2)}, u32[]{:S(2)}) collective-permute-start(bf16[512,128]{0,1:T(8,128)(2,1)} %get-tuple-element.28), channel_id=1, source_target_pairs={{0,8},{8,16},{16,24},{24,32},{32,40},{40,48},{48,56},{56,64},{64,7... | collective-permute-start | bytes 393224 | tf_op jit(solution)/shard_map/ppermute | solution.py:34
  75.2 5.1 %copy-start.19 = (f32[1,128,128]{2,1,0:T(8,128)S(1)}, f32[1,128,128]{2,1,0:T(8,128)}, u32[]{:S(2)}) copy-start(f32[1,128,128]{2,1,0:T(8,128)} %convolution_bitcast_fusion.1) | copy-start | bytes 196612
  75.2 5.2 %copy-start.22 = (f32[1,128,128]{2,1,0:T(8,128)S(1)}, f32[1,128,128]{2,1,0:T(8,128)}, u32[]{:S(2)}) copy-start(f32[1,128,128]{2,1,0:T(8,128)} %convolution_bitcast_fusion.2) | copy-start | bytes 196612
  75.2 5.9 %copy-start.2 = (f32[1024,128]{1,0:T(8,128)S(1)}, f32[1024,128]{1,0:T(8,128)}, u32[]{:S(2)}) copy-start(f32[1024,128]{1,0:T(8,128)} %convolution_add_fusion.1) | copy-start | bytes 1572868
  80.0 391.7 %all-reduce.5.cloned.1.call-start = ((), (), s32[]{:S(2)}) async-start(), calls=%async_computation.1 | async-start | bytes 393216 | tf_op jit(solution)/shard_map/psum | solution.py:148
  (15 other events, 47.6 us)
Sparse Core Ops, SparseCore 0:
  80.1 115.9 all-reduce.2
  201.6 270.0 all-reduce.4
where the time goes:
time: 481 us; the launch traced here: 480 us
  waiting for transfers between devices  393 us (82%)
  matrix products  29.5 us (6%)
  starting transfers between devices  29 us (6%)
  between operations  14.6 us (3%)
  local copies, waits for them, and re-layouts  9.33 us (2%)
    psum x1, waiting for transfers between devices, body(): weight_grad = lax.psum(partial_mix, ('node', 'win'))  274 us
    psum x1, waiting for transfers between devices, body(): lax.psum(jnp.concatenate([source_grad, target_grad], axis=1).astype(jnp.b...  113 us
    ppermute x4, starting transfers between devices, shifted(): return lax.ppermute(block, axis, route)  12 us
    ppermute x2, starting transfers between devices, padded(): lax.ppermute(head, axis, [((i + 1) % count, i) for i in range(ends)])  10.7 us
  transfers between devices with their start and end apart: 10, of which 6 were waited for; matrix products, arithmetic and copies ran while one was open for 3% of the time, Pallas kernels for 0%

commit v1 on v0

--- a/solution.py
+++ b/solution.py
@@ -145,7 +145,7 @@
         )
         * norm_scale
     )
-    weight_grad = lax.psum(partial_mix, ("node", "win"))
+    weight_grad = lax.psum(lax.psum(partial_mix, "node"), "win")
     back_two = lax.dot_general(
         upstream, mix_weight[2], ROWS_DIMS, preferred_element_type=jnp.float32
     ).reshape(node_count, row_width)

time: 481 us -> 800 us (1.66)
  waiting for transfers between devices: 393 us -> 708 us
    psum x1 -> x2, waiting for transfers between devices: 274 us -> 597 us  [body(): weight_grad = lax.psum(lax.psum(partial_mix, 'node'), 'win')]
  transfers between devices with their start and end apart: 10 -> 11, of which waited for: 6 -> 6; matrix products, arithmetic and copies ran while one was open for 3% -> 2% of each run, Pallas kernels for 0% -> 0%
where the time goes in v1:
time: 800 us; the launch traced here: 795 us
  waiting for transfers between devices  708 us (88%)
  starting transfers between devices  29.3 us (4%)
  matrix products  29 us (4%)
  between operations  14.2 us (2%)
  local copies, waits for them, and re-layouts  10.3 us (1%)
    psum x2, waiting for transfers between devices, body(): weight_grad = lax.psum(lax.psum(partial_mix, 'node'), 'win')  597 us
    psum x1, waiting for transfers between devices, body(): lax.psum(jnp.concatenate([source_grad, target_grad], axis=1).astype(jnp.b...  106 us
  transfers between devices with their start and end apart: 11, of which 6 were waited for; matrix products, arithmetic and copies ran while one was open for 2% of the time, Pallas kernels for 0%

profile of v1, /device:TPU:1, one launch (start us, length us, event | category | flops | bytes accessed | tf_op | source)
XLA Modules:
  0.0 795.0 jit_solution(5362295032494315795)
XLA Ops:
  7.2 2.2 fusion.88
  9.4 2.1 fusion.83
  12.9 8.7 %collective-permute-start.1 = (bf16[512,384]{1,0:T(8,128)(2,1)S(1)}, bf16[512,384]{1,0:T(8,128)(2,1)S(1)}, u32[]{:S(2)}, u32[]{:S(2)}) collective-permute-start(bf16[512,384]{1,0:T(8,128)(2,1)S(1)} %pad_maximum_fusion.1), channel_id=1, source_target_pairs={{8,0},{16,8},{24,16},{32,24},{40,32},{48,40},{56,48},{64,56},{72,6... | collective-permute-start | bytes 1179656 | tf_op jit(solution)/shard_map/ppermute | solution.py:24
  21.6 1.9 collective-permute-start
  25.0 3.2 collective-permute-done
  28.7 3.3 fusion.6
  32.0 1.4 add_convert_fusion.2
  33.5 1.9 collective-permute-start.3
  35.4 4.4 collective-permute-start.2
  43.1 3.6 multiply_reduce_fusion
  48.2 1.9 collective-permute-start.4
  50.1 4.3 collective-permute-start.5
  58.4 1.6 multiply_reduce_fusion.1
  60.0 4.0 fusion.5
  64.1 1.3 fusion.90
  66.0 1.9 collective-permute-start.6
  68.0 4.0 collective-permute-start.7
  74.3 1.9 fusion.31
  80.3 487.6 %all-reduce.6.cloned.1.call-done = f32[3,128,128]{2,1,0:T(8,128)} async-done(((f32[3,128,128]{2,1,0:T(8,128)}), f32[3,128,128]{2,1,0:T(8,128)}) %all-reduce.6.cloned.1.call-update) | async-done | bytes 196624 | tf_op jit(solution)/shard_map/psum | solution.py:148
  568.0 1.7 fusion.14
  569.7 106.3 %all-reduce.4.cloned.1.call-done = bf16[512,128]{0,1:T(8,128)(2,1)} async-done(((bf16[512,128]{0,1:T(8,128)(2,1)}), bf16[512,128]{0,1:T(8,128)(2,1)}) %all-reduce.4.cloned.1.call-update) | async-done | bytes 131088 | tf_op jit(solution)/shard_map/psum | solution.py:193
  676.0 1.7 copy.38
  677.7 109.2 %all-reduce.8.cloned.1.call-done = f32[3,128,128]{2,1,0:T(8,128)} async-done(((f32[3,128,128]{2,1,0:T(8,128)}), f32[3,128,128]{2,1,0:T(8,128)}) %all-reduce.8.cloned.1.call-update) | async-done | bytes 196624 | tf_op jit(solution)/shard_map/psum | solution.py:148
  786.9 1.6 copy.55
  (94 shorter events, 18.8 us)
Async XLA Ops:
  7.2 17.6 %copy-start = (bf16[512,1,2,128]{3,2,1,0:T(2,128)(2,1)S(1)}, bf16[512,1,2,128]{3,2,1,0:T(2,128)(2,1)}, u32[]{:S(2)}) copy-start(bf16[512,1,2,128]{3,2,1,0:T(2,128)(2,1)} %param.11) | copy-start | bytes 786436
  7.2 16.4 %copy-start.20 = (s32[128]{0:T(128)S(1)}, s32[128]{0:T(128)}, u32[]{:S(2)}) copy-start(s32[128]{0:T(128)} %param.10) | copy-start | bytes 1540
  7.2 17.6 %copy-start.11 = (bf16[3,128,128]{2,1,0:T(8,128)(2,1)S(1)}, bf16[3,128,128]{2,1,0:T(8,128)(2,1)}, u32[]{:S(2)}) copy-start(bf16[3,128,128]{2,1,0:T(8,128)(2,1)} %param.9) | copy-start | bytes 294916
  7.2 560.8 %all-reduce.6.cloned.1.call-start = ((), (), s32[]{:S(2)}) async-start(), calls=%async_computation.1 | async-start | bytes 393216 | tf_op jit(solution)/shard_map/psum | solution.py:148
  9.4 19.2 %copy-start.9 = (bf16[512,64]{0,1:T(8,128)(2,1)}, bf16[512,64]{0,1:T(8,128)(2,1)S(1)}, u32[]{:S(2)}) copy-start(bf16[512,64]{0,1:T(8,128)(2,1)S(1)} %get-tuple-element.29) | copy-start | bytes 196612
  12.9 12.2 %collective-permute-start.1 = (bf16[512,384]{1,0:T(8,128)(2,1)S(1)}, bf16[512,384]{1,0:T(8,128)(2,1)S(1)}, u32[]{:S(2)}, u32[]{:S(2)}) collective-permute-start(bf16[512,384]{1,0:T(8,128)(2,1)S(1)} %pad_maximum_fusion.1), channel_id=1, source_target_pairs={{8,0},{16,8},{24,16},{32,24},{40,32},{48,40},{56,48},{64,56},{72,6... | collective-permute-start | bytes 1179656 | tf_op jit(solution)/shard_map/ppermute | solution.py:24
  21.6 6.6 collective-permute-start
  28.4 26.9 %copy-start.1 = (bf16[1536,384]{1,0:T(8,128)(2,1)}, bf16[1536,384]{1,0:T(8,128)(2,1)S(1)}, u32[]{:S(2)}) copy-start(bf16[1536,384]{1,0:T(8,128)(2,1)S(1)} %pad_maximum_fusion) | copy-start | bytes 3538948
  33.5 13.3 %copy-start.14 = (bf16[512,256]{1,0:T(8,128)(2,1)}, bf16[512,256]{1,0:T(8,128)(2,1)S(1)}, u32[]{:S(2)}) copy-start(bf16[512,256]{1,0:T(8,128)(2,1)S(1)} %get-tuple-element.33) | copy-start | bytes 786436
  33.5 9.5 %collective-permute-start.3 = (bf16[512,256]{1,0:T(8,128)(2,1)S(1)}, bf16[512,256]{1,0:T(8,128)(2,1)S(1)}, u32[]{:S(2)}, u32[]{:S(2)}) collective-permute-start(bf16[512,256]{1,0:T(8,128)(2,1)S(1)} %get-tuple-element.33), channel_id=1, source_target_pairs={{8,0},{16,8},{24,16},{32,24},{40,32},{48,40},{56,48},{64,56},{72,6... | collective-permute-start | bytes 786440 | tf_op jit(solution)/shard_map/ppermute | solution.py:24
  35.4 7.7 collective-permute-start.2
  48.2 10.2 %collective-permute-start.4 = (bf16[512,256]{1,0:T(8,128)(2,1)}, bf16[512,256]{1,0:T(8,128)(2,1)}, u32[]{:S(2)}, u32[]{:S(2)}) collective-permute-start(bf16[512,256]{1,0:T(8,128)(2,1)} %get-tuple-element.24), channel_id=1, source_target_pairs={{8,0},{16,8},{24,16},{32,24},{40,32},{48,40},{56,48},{64,56},{72,6... | collective-permute-start | bytes 786440 | tf_op jit(solution)/shard_map/ppermute | solution.py:34
  50.1 8.3 %collective-permute-start.5 = (bf16[512,256]{1,0:T(8,128)(2,1)}, bf16[512,256]{1,0:T(8,128)(2,1)}, u32[]{:S(2)}, u32[]{:S(2)}) collective-permute-start(bf16[512,256]{1,0:T(8,128)(2,1)} %get-tuple-element.25), channel_id=1, source_target_pairs={{0,8},{8,16},{16,24},{24,32},{32,40},{40,48},{48,56},{56,64},{64,7... | collective-permute-start | bytes 786440 | tf_op jit(solution)/shard_map/ppermute | solution.py:34
  55.3 4.7 copy-start.18
  55.3 4.7 slice-start
  60.0 4.0 copy-start.10
  64.0 8.3 %copy-start.15 = (f32[1,128,128]{2,1,0:T(8,128)S(1)}, f32[1,128,128]{2,1,0:T(8,128)}, u32[]{:S(2)}) copy-start(f32[1,128,128]{2,1,0:T(8,128)} %convolution_bitcast_fusion.1) | copy-start | bytes 196612
  64.0 8.3 %copy-start.17 = (f32[1,128,128]{2,1,0:T(8,128)S(1)}, f32[1,128,128]{2,1,0:T(8,128)}, u32[]{:S(2)}) copy-start(f32[1,128,128]{2,1,0:T(8,128)} %convolution_bitcast_fusion.2) | copy-start | bytes 196612
  64.0 10.2 %copy-start.4 = (bf16[1536,64]{1,0:T(8,128)(2,1)S(1)}, bf16[1536,64]{1,0:T(8,128)(2,1)}, u32[]{:S(2)}) copy-start(bf16[1536,64]{1,0:T(8,128)(2,1)} %copy-done.3) | copy-start | bytes 589828
  66.0 7.0 collective-permute-start.6
  68.0 6.3 collective-permute-start.7
  72.3 7.0 copy-start.2
  73.0 602.9 %all-reduce.4.cloned.1.call-start = ((), (), s32[]{:S(2)}) async-start(), calls=%async_computation | async-start | bytes 262144 | tf_op jit(solution)/shard_map/psum | solution.py:193
  79.3 707.6 %all-reduce.8.cloned.1.call-start = ((), (), s32[]{:S(2)}) async-start(), calls=%async_computation.2 | async-start | bytes 393216 | tf_op jit(solution)/shard_map/psum | solution.py:148
  (10 other events, 29.7 us)
Sparse Core Ops, SparseCore 0:
  73.2 494.7 all-reduce.5
  571.4 104.4 all-reduce.3
  678.9 107.9 all-reduce.7
